TPU v7x, 32 devices: a whole 2x2x4 slice. The times are simulated.
32 devices in a mesh: week: 4 (over x, core), row: 4 (over z), col: 2 (over y).
Axes of the slice: x: 2, y: 2, z: 4, core: 2. Of those that a mesh axis runs over, the one named last changes fastest.
Arguments:
- sensitivity: bfloat16 [4, 3, 1024, 4096], P('week', None, None, ('row', 'col')), may hold values from -0.1875 to 0.1875
- reach: int32 [4, 1024], P('week'), may hold values from 0 to 2, as said below
- obs_weight: float32 [4, 1024], P('week'), may hold values from 0.25 to 4
- prior_precision: float32 [4, 4096], P('week', ('row', 'col')), may hold values from 0.5 to 4
- pivot_solve: bfloat16 [4096, 4096], P('week', ('row', 'col')), may hold values from -0.09375 to 0.09375
Outputs:
- hessian_band: float32 [4, 3, 4096, 4096], P('week', None, ('row', 'col'))
- panel: bfloat16 [4096, 4096], P(('row', 'col'), 'week')
- schur: float32 [4096, 4096], P(('row', 'col'), 'week')
Inputs may be any that keep to these rules, and one draw needn't show every extreme that they name: The number of observations at each reach differs widely from week to week; in some week w >= 2 every observation has reach 2.
All inputs are finite; a program needn't handle non-finite values.
Results may differ from a plain program's by a relative error of at most 0.013.
Values may be sent and summed in bfloat16 or wider, within the bound.
A program may use at most 128 MiB of HBM per device.

v0:
```python
import jax
import jax.numpy as jnp
from jax import lax
from jax.sharding import PartitionSpec as P


def from_behind(block, axis, distance):
    devices = range(lax.axis_size(axis))
    route = [(i - distance, i) for i in devices if i - distance in devices]
    return lax.ppermute(block, axis, route)


def spread(shard, axis, root):
    mine = lax.axis_index(axis) == root
    return lax.psum(jnp.where(mine, shard, jnp.zeros_like(shard)), axis)


def contract_first(left, right):
    return lax.dot_general(
        left, right, (((0,), (0,)), ((), ())), preferred_element_type=jnp.float32
    )


def contract_last(left, right):
    return lax.dot_general(
        left, right, (((1,), (1,)), ((), ())), preferred_element_type=jnp.float32
    )


def lag_pairs(firsts, lags):
    return [(a, b) for a in firsts for b in range(a, lags)]


def weighted(source, offset, pairs, reach_here, weight_here, week_of):
    result = []
    for a, b in pairs:
        keep = jnp.where((reach_here >= b) & (week_of >= b), weight_here, 0.0)
        result.append((keep[:, None] * source[a - offset].astype(jnp.float32)).astype(jnp.bfloat16))
    return result


def products(lefts, right, offset, pairs):
    result = []
    for position in range(len(pairs)):
        result.append(contract_first(lefts[position], right[pairs[position][1] - offset]))
    return jnp.stack(result)


def body(sensitivity, reach, obs_weight, prior_precision, pivot_solve):
    week = lax.axis_index("week")
    n_row = lax.axis_size("row")
    n_col = lax.axis_size("col")
    local = sensitivity[0]
    lags = local.shape[0]
    slim = local.shape[2]
    regions = slim * n_row * n_col
    reach_here = reach[0]
    weight_here = obs_weight[0]
    starts = [sum((lags - k for k in range(a))) for a in range(lags)]
    local_pairs = lag_pairs(range(lags), lags)
    lefts = weighted(local, 0, local_pairs, reach_here, weight_here, week)
    partial_blocks = products(
        lefts, lax.all_gather(local, ("row", "col"), axis=2, tiled=True), 0, local_pairs
    )
    carried = []
    for a in range(lags - 1, 0, -1):
        outgoing = partial_blocks[starts[a] : starts[a] + lags - a]
        if len(carried) > 0:
            outgoing = outgoing.at[: lags - a - 1].add(carried[0])
        carried = [from_behind(outgoing.astype(jnp.bfloat16), "week", -1).astype(outgoing.dtype)]
    bands = partial_blocks[0:lags].at[: lags - 1].add(carried[0])
    first_row = (lax.axis_index("row") * n_col + lax.axis_index("col")) * slim
    row_ids = lax.broadcasted_iota(jnp.int32, (slim, regions), 0)
    col_ids = lax.broadcasted_iota(jnp.int32, (slim, regions), 1)
    diagonal = jnp.where(col_ids == row_ids + first_row, prior_precision[0][:, None], 0.0)
    bands = bands.at[0].add(diagonal)
    coupling = spread(bands[1].astype(jnp.bfloat16), "week", 1)
    panel_sum = contract_last(
        coupling, lax.all_gather(pivot_solve, ("row", "col"), axis=1, tiled=True)
    )
    panel = panel_sum.astype(jnp.bfloat16)
    gram = contract_last(panel, lax.all_gather(panel, ("row", "col"), axis=0, tiled=True))
    term = jnp.where(week == 1, bands[0], 0.0) - gram
    schur = lax.psum_scatter(
        term.astype(jnp.bfloat16), "week", scatter_dimension=1, tiled=True
    ).astype(jnp.float32)
    return (bands[None], panel, schur)


def solution(mesh):
    placed = (
        P("week", None, None, ("row", "col")),
        P("week", None),
        P("week", None),
        P("week", ("row", "col")),
        P("week", ("row", "col")),
    )
    return jax.shard_map(
        body,
        mesh=mesh,
        in_specs=placed,
        out_specs=(
            P("week", None, ("row", "col"), None),
            P(("row", "col"), "week"),
            P(("row", "col"), "week"),
        ),
        check_vma=False,
    )
```

profile of v0, /device:TPU:0, one launch (start us, length us, event | category | flops | bytes accessed | tf_op | source)
XLA Modules:
  0.0 967.8 jit_solution(10031610133609217427)
XLA Ops:
  8.0 0.7 and_select_fusion.2
  8.7 484.0 %all-gather.9.cloned.1.call-done = bf16[1,3,1024,4096]{3,2,1,0:T(8,128)(2,1)} async-done(((bf16[1,3,1024,512]{3,2,1,0:T(8,128)(2,1)}), bf16[1,3,1024,4096]{3,2,1,0:T(8,128)(2,1)}) %all-gather.9.cloned.1.call-update) | async-done | bytes 25165840 | tf_op jit(solution)/shard_map/all_gather | solution.py:63
  492.6 10.5 %fusion.10 = bf16[1,512,4096]{2,1,0:T(8,128)(2,1)} fusion(bf16[1,3,1024,4096]{3,2,1,0:T(8,128)(2,1)} %all-gather.9.cloned.1.call-done, bf16[1,3,1024,512]{3,2,1,0:T(8,128)(2,1)} %param.11, f32[1024]{0:T(1024)S(1)} %bitcast.71), kind=kOutput, calls=%fused_computation.23 | convolution fusion | flops 4298637312 | bytes 13635584 | tf_op jit(solution)/shard_map/dot_general | solution.py:19
  503.1 1.3 collective-permute-start
  504.5 9.7 %convolution_bitcast_fusion = bf16[1,512,4096]{2,1,0:T(8,128)(2,1)} fusion(bf16[1,3,1024,4096]{3,2,1,0:T(8,128)(2,1)} %all-gather.9.cloned.1.call-done, f32[1024]{0:T(1024)S(1)} %bitcast.72, bf16[1,3,1024,512]{3,2,1,0:T(8,128)(2,1)S(1)} %copy-done), kind=kOutput, calls=%fused_computation.18 | convolution fusion | flops 4296540160 | bytes 13635584 | tf_op jit(solution)/shard_map/dot_general | solution.py:19
  514.2 11.0 %fusion.5 = f32[1,512,4096]{2,1,0:T(8,128)} fusion(bf16[1,3,1024,4096]{3,2,1,0:T(8,128)(2,1)} %all-gather.9.cloned.1.call-done, f32[1024]{0:T(1024)S(1)} %bitcast.68, bf16[1,3,1024,512]{3,2,1,0:T(8,128)(2,1)S(1)} %copy-done), kind=kOutput, calls=%fused_computation.16 | convolution fusion | flops 4296540160 | bytes 17829888 | tf_op jit(solution)/shard_map/dot_general | solution.py:19
  525.2 8.7 pad_maximum_fusion.1
  533.9 8.1 add_dynamic-update-slice_fusion
  542.0 1.5 collective-permute-start.1
  543.5 7.2 fusion.4
  550.7 7.5 convolution_bitcast_fusion.1
  558.2 7.7 fusion.6
  566.0 8.9 pad_maximum_fusion
  574.9 1.4 collective-permute-done.1
  576.3 14.8 %constant_dynamic-update-slice_fusion = (f32[3,512,4096]{2,1,0:T(8,128)}, f32[2,512,4096]{2,1,0:T(8,128)}) fusion(f32[3,512,4096]{2,1,0:T(8,128)} %pad_maximum_fusion, bf16[2,512,4096]{2,1,0:T(8,128)(2,1)} %collective-permute-done.1, f32[1,512,4096]{2,1,0:T(8,128)S(1)} %fusion.4, f32[1,512,4096]{2,1,0:T(8,128)S(1)} %fusion.6), kind=kLoop, calls=%fused_computation.60 | loop fusion | flops 12582912 | bytes 58720256 | tf_op jit(solution)/shard_map/scatter-add | solution.py:71
  591.1 6.5 fusion.8
  597.6 5.8 fusion.12
  603.6 28.6 %all-gather.5.cloned.1.call-done = bf16[1024,4096]{1,0:T(8,128)(2,1)} async-done(((bf16[1024,512]{1,0:T(8,128)(2,1)}), bf16[1024,4096]{1,0:T(8,128)(2,1)}) %all-gather.5.cloned.1.call-update) | async-done | bytes 8388624 | tf_op jit(solution)/shard_map/all_gather | solution.py:79
  632.2 135.7 %all-reduce.2.cloned.1.call-done = bf16[512,4096]{1,0:T(8,128)(2,1)} async-done(((bf16[512,4096]{1,0:T(8,128)(2,1)}), bf16[512,4096]{1,0:T(8,128)(2,1)}) %all-reduce.2.cloned.1.call-update) | async-done | bytes 4194320 | tf_op jit(solution)/shard_map/psum | solution.py:15
  767.9 10.1 %convolution_convert_fusion = bf16[512,1024]{1,0:T(8,128)(2,1)} fusion(bf16[512,4096]{1,0:T(8,128)(2,1)} %all-reduce.2.cloned.1.call-done, bf16[1024,4096]{1,0:T(8,128)(2,1)} %all-gather.5.cloned.1.call-done), kind=kOutput, calls=%fused_computation.37 | convolution fusion | flops 4295491584 | bytes 13631488 | tf_op jit(solution)/shard_map/dot_general | solution.py:25
  778.1 124.7 %all-gather.7.cloned.1.call-done = bf16[4096,1024]{1,0:T(8,128)(2,1)} async-done(((bf16[512,1024]{1,0:T(8,128)(2,1)}), bf16[4096,1024]{1,0:T(8,128)(2,1)}) %all-gather.7.cloned.1.call-update) | async-done | bytes 8388624 | tf_op jit(solution)/shard_map/all_gather | solution.py:82
  902.8 12.9 %fusion.1 = bf16[512,4096]{1,0:T(8,128)(2,1)} fusion(f32[2,512,4096]{2,1,0:T(8,128)} %get-tuple-element.40, bf16[512,1024]{1,0:T(8,128)(2,1)} %convolution_convert_fusion, bf16[4096,1024]{1,0:T(8,128)(2,1)} %all-gather.7.cloned.1.call-done, f32[512]{0:T(512)S(1)} %bitcast.75, s32[512]{0:T(512)S(1)} %iota_add_fusion, pred[]{:T(512)S(6)} %eq.13), kind=kOutput, calls=%fused_computation.10 | convolution fusion | flops 4307550208 | bytes 22024192 | tf_op jit(solution)/shard_map/dot_general | solution.py:25
  915.7 42.7 %reduce-scatter.2.cloned.1.call-done = bf16[512,1024]{1,0:T(8,128)(2,1)} async-done(((bf16[512,4096]{1,0:T(8,128)(2,1)}), bf16[512,1024]{1,0:T(8,128)(2,1)}) %reduce-scatter.2.cloned.1.call-update) | async-done | bytes 1048592 | tf_op jit(solution)/shard_map/reduce_scatter | solution.py:84
  958.4 2.8 convert_element_type.102
  (16 shorter events, 1.2 us)
Async XLA Ops:
  7.2 485.5 %all-gather.9.cloned.1.call-start = ((), (), s32[]{:S(2)}) async-start(), calls=%async_computation.5 | async-start | bytes 28311552 | tf_op jit(solution)/shard_map/all_gather | solution.py:63
  7.9 624.3 %all-gather.5.cloned.1.call-start = ((), (), s32[]{:S(2)}) async-start(), calls=%async_computation.2 | async-start | bytes 9437184 | tf_op jit(solution)/shard_map/all_gather | solution.py:79
  492.6 11.8 %copy-start = (bf16[1,3,1024,512]{3,2,1,0:T(8,128)(2,1)S(1)}, bf16[1,3,1024,512]{3,2,1,0:T(8,128)(2,1)}, u32[]{:S(2)}) copy-start(bf16[1,3,1024,512]{3,2,1,0:T(8,128)(2,1)} %param.11) | copy-start | bytes 9437188
  503.1 30.8 %collective-permute-start = (bf16[1,512,4096]{2,1,0:T(8,128)(2,1)}, bf16[1,512,4096]{2,1,0:T(8,128)(2,1)}, u32[]{:S(2)}, u32[]{:S(2)}) collective-permute-start(bf16[1,512,4096]{2,1,0:T(8,128)(2,1)} %fusion.10), channel_id=1, source_target_pairs={{8,0},{16,8},{24,16},{9,1},{17,9},{25,17},{10,2},{18,10},{26,18},{... | collective-permute-start | bytes 12582920 | tf_op jit(solution)/shard_map/ppermute | solution.py:10
  504.4 263.4 %all-reduce.2.cloned.1.call-start = ((), (), s32[]{:S(2)}) async-start(), calls=%async_computation.1 | async-start | bytes 8388608 | tf_op jit(solution)/shard_map/psum | solution.py:15
  542.0 34.3 %collective-permute-start.1 = (bf16[2,512,4096]{2,1,0:T(8,128)(2,1)}, bf16[2,512,4096]{2,1,0:T(8,128)(2,1)}, u32[]{:S(2)}, u32[]{:S(2)}) collective-permute-start(bf16[2,512,4096]{2,1,0:T(8,128)(2,1)} %add_dynamic-update-slice_fusion), channel_id=1, source_target_pairs={{8,0},{16,8},{24,16},{9,1},{17,9},{25,17},{10,2},{18,10},{26,18},{... | collective-permute-start | bytes 25165832 | tf_op jit(solution)/shard_map/ppermute | solution.py:10
  574.9 16.2 %copy-start.1 = (f32[1,512]{1,0:T(1,128)S(1)}, f32[1,512]{1,0:T(1,128)}, u32[]{:S(2)}) copy-start(f32[1,512]{1,0:T(1,128)} %param.14) | copy-start | bytes 6148
  603.4 299.4 %all-gather.7.cloned.1.call-start = ((), (), s32[]{:S(2)}) async-start(), calls=%async_computation.3 | async-start | bytes 9437184 | tf_op jit(solution)/shard_map/all_gather | solution.py:82
  778.0 180.4 %reduce-scatter.2.cloned.1.call-start = ((), (), s32[]{:S(2)}) async-start(), calls=%async_computation.4 | async-start | bytes 5242880 | tf_op jit(solution)/shard_map/reduce_scatter | solution.py:84
Sparse Core Ops, SparseCore 0:
  9.5 483.0 all-gather.8
  504.5 127.5 all-gather.4
  634.5 133.2 all-reduce.1
  778.2 124.6 all-gather.6
  915.8 42.5 reduce-scatter.1
where the time goes:
time: 968 us
  waiting for transfers between devices  818 us (85%)
  matrix products  76.6 us (8%)
  other arithmetic  56.3 us (6%)
  between operations  13.9 us (1%)
    all_gather x1, waiting for transfers between devices, body(): lax.all_gather(local, ('row', 'col'), axis=2, tiled=True)  484 us
    psum x1, waiting for transfers between devices, spread(): return lax.psum(jnp.where(mine, shard, jnp.zeros_like(shard)), axis)  136 us
    all_gather x1, waiting for transfers between devices, body(): lax.all_gather(panel, ('row', 'col'), axis=0, tiled=True)  125 us
    dot_general x6, matrix products, contract_first(): lax.dot_general(left, right, (((0,), (0,)), ((), ())), preferred_element_...  53.6 us
    reduce_scatter x1, waiting for transfers between devices, body(): lax.psum_scatter(term.astype(jnp.bfloat16), 'week', scatter_dimension=1,...  42.7 us
    all_gather x1, waiting for transfers between devices, body(): lax.all_gather(pivot_solve, ('row', 'col'), axis=1, tiled=True)  28.6 us
    dot_general x2, matrix products, contract_last(): lax.dot_general(left, right, (((1,), (1,)), ((), ())), preferred_element_...  23 us
  transfers between devices with their start and end apart: 7, of which 6 were waited for; matrix products, arithmetic and copies ran while one was open for 10% of the time, Pallas kernels for 0%

commit v1 on v0

v1 whole, which is shorter than its diff:
```python
import functools

import jax
import jax.numpy as jnp
from jax import lax
from jax.experimental import pallas as pl
from jax.experimental.pallas import tpu as pltpu
from jax.sharding import PartitionSpec as P

ROW, COL = "row", "col"


def gather_kernel(n_row, n_col, axis, by_week, x_ref, out_ref, own, ring_s, ring_r, mid_s, mid_r,
                  side_s, side_r, pass_s, pass_r, own_sem):
    row, col = lax.axis_index(ROW), lax.axis_index(COL)
    week = lax.axis_index("week")
    parts, length, width = x_ref.shape
    half = length // 2
    band = (3 * half // 16) // 16 * 16
    up = lax.rem(row + 1, n_row)
    down = lax.rem(row + n_row - 1, n_row)
    ends = ((up, 0), (down, half))
    step_size = width if axis == 2 else length

    barrier = pltpu.get_barrier_semaphore()
    for target in (up, down):
        pl.semaphore_signal(barrier, inc=1, device_id={ROW: target})
    for k in range(1, n_col):
        pl.semaphore_signal(barrier, inc=1, device_id={COL: lax.rem(col + k, n_col)})
    pl.semaphore_wait(barrier, 2 + n_col - 1)

    def place(part, at_row, at_col, first, count):
        start = pl.multiple_of((at_row * n_col + at_col) * step_size, step_size)
        if axis == 2:
            return out_ref.at[part, pl.ds(first, count), pl.ds(start, width)]
        return out_ref.at[part, pl.ds(pl.multiple_of(start + first, 16), count), :]

    def source(part, first, count):
        return x_ref.at[part, pl.ds(first, count), :]

    def origin(step, d):
        return lax.rem(row + (n_row - step if d == 0 else step), n_row)

    def ring(part, step, d, at_col):
        first = ends[d][1]
        at = origin(step, d)
        src = source(part, first, half) if step == 0 else place(part, at, at_col, first, half)
        return pltpu.make_async_remote_copy(
            src, place(part, at, at_col, first, half),
            ring_s.at[part, step, d], ring_r.at[part, step, d], device_id={ROW: ends[d][0]})

    def mid(part, step, d, k):
        first = half - band if d == 0 else half
        at = origin(step, d)
        ref = place(part, at, lax.rem(col + n_col - k, n_col), first, band)
        return pltpu.make_async_remote_copy(
            ref, ref, mid_s.at[part, step, d, k - 1], mid_r.at[part, step, d, k - 1],
            device_id={ROW: ends[d][0]})

    pieces = ((half - band, 2 * band), (0, half - band), (half + band, half - band))

    def side(part, piece, k):
        first, count = pieces[piece]
        return pltpu.make_async_remote_copy(
            source(part, first, count), place(part, row, col, first, count),
            side_s.at[part, piece, k - 1], side_r.at[part, piece, k - 1],
            device_id={COL: lax.rem(col + k, n_col)})

    def onward(part, step, d, k):
        first, count = pieces[1 + d]
        ref = place(part, origin(step, d), col, first, count)
        return pltpu.make_async_remote_copy(
            ref, ref, pass_s.at[part, step - 1, d, k - 1], pass_r.at[part, step - 1, d, k - 1],
            device_id={COL: lax.rem(col + k, n_col)})

    def each(body):
        for part in range(parts):
            if by_week and part > 0:
                pl.when(week >= part)(functools.partial(body, part))
            else:
                body(part)

    peers = range(1, n_col)

    def take_own(part):
        return pltpu.make_async_copy(x_ref.at[part], own.at[part], own_sem.at[part])

    def put_own(part):
        return pltpu.make_async_copy(own.at[part], place(part, row, col, 0, length), own_sem.at[part])

    def begin(part):
        for d in range(2):
            ring(part, 0, d, col).start()
        for k in peers:
            side(part, 0, k).start()
        for k in peers:
            side(part, 1, k).start()
            side(part, 2, k).start()
        take_own(part).start()

    each(begin)

    def spread_mid(part):
        take_own(part).wait()
        put_own(part).start()
        for k in peers:
            side(part, 0, k).wait_recv()
            for d in range(2):
                mid(part, 0, d, k).start()

    each(spread_mid)
    for step in range(1, n_row):
        def advance(part, step=step):
            for d in range(2):
                ring(part, step - 1, d, col).wait_recv()
                if step < n_row - 1:
                    ring(part, step, d, col).start()
                for k in peers:
                    onward(part, step, d, k).start()
                for k in peers:
                    mid(part, step - 1, d, k).wait_recv()
                    if step < n_row - 1:
                        mid(part, step, d, k).start()

        each(advance)

    def finish(part):
        put_own(part).wait()
        for k in peers:
            side(part, 0, k).wait_send()
            side(part, 1, k).wait()
            side(part, 2, k).wait()
        for step in range(n_row - 1):
            for d in range(2):
                ring(part, step, d, col).wait_send()
                for k in peers:
                    mid(part, step, d, k).wait_send()
                    onward(part, step + 1, d, k).wait()

    each(finish)


def gather(x, axis, by_week, collective_id):
    n_row, n_col = lax.axis_size(ROW), lax.axis_size(COL)
    parts, length, width = x.shape
    n = n_row * n_col
    shape = (parts, length, width * n) if axis == 2 else (parts, length * n, width)
    dma = pltpu.SemaphoreType.DMA
    ring_sems = dma((parts, n_row - 1, 2))
    mid_sems = dma((parts, n_row - 1, 2, n_col - 1))
    side_sems = dma((parts, 3, n_col - 1))
    sent = x.size * 2 * (n - 1)
    return pl.pallas_call(
        functools.partial(gather_kernel, n_row, n_col, axis, by_week),
        out_shape=jax.ShapeDtypeStruct(shape, x.dtype),
        in_specs=[pl.BlockSpec(memory_space=pl.ANY)],
        out_specs=pl.BlockSpec(memory_space=pl.ANY),
        scratch_shapes=[
            pltpu.VMEM(x.shape, x.dtype),
            ring_sems, ring_sems, mid_sems, mid_sems, side_sems, side_sems, mid_sems, mid_sems,
            dma((parts,)),
        ],
        compiler_params=pltpu.CompilerParams(collective_id=collective_id, has_side_effects=True),
        cost_estimate=pl.CostEstimate(flops=0, bytes_accessed=sent * 8, transcendentals=0),
    )(x)


def send(block, moves):
    return lax.ppermute(block.astype(jnp.bfloat16), "week", moves)


def contract_first(left, right):
    return lax.dot_general(
        left, right, (((0,), (0,)), ((), ())), preferred_element_type=jnp.float32
    )


def contract_last(left, right):
    return lax.dot_general(
        left, right, (((1,), (1,)), ((), ())), preferred_element_type=jnp.float32
    )


def body(sensitivity, reach, obs_weight, prior_precision, pivot_solve):
    week = lax.axis_index("week")
    n_week, n_row, n_col = (lax.axis_size(name) for name in ("week", ROW, COL))
    local = sensitivity[0]
    slim = local.shape[2]
    regions = slim * n_row * n_col
    full = gather(local, 2, True, 0)

    def product(a, b):
        keep = jnp.where((reach[0] >= b) & (week >= b), obs_weight[0], 0.0)
        left = (keep[:, None] * local[a].astype(jnp.float32)).astype(jnp.bfloat16)
        return jnp.where(week >= b, contract_first(left, full[b]), 0.0)

    down = [(w, w - 1) for w in range(1, n_week)]
    late = [(w, w - 1) for w in range(2, n_week)]
    p11 = product(1, 2).astype(jnp.bfloat16)
    from_later = send(p11, late)
    p01 = product(0, 1)
    from_earlier = send(p01, [(1, 2)])
    h1 = p01 + from_later.astype(jnp.float32)
    mine = jnp.where(
        week == 1, h1, from_earlier.astype(jnp.float32) + p11.astype(jnp.float32)
    ).astype(jnp.bfloat16)
    moves = [[(2, w)] for w in range(3, n_week)]
    moves[0].append((1, 0))
    coupling = jnp.where((week == 1) | (week == 2), mine, 0)
    for move in moves:
        coupling = coupling + send(mine, move)

    p20 = send(product(2, 2), late)
    p10 = send(product(1, 1) + p20.astype(jnp.float32), down)
    first_row = (lax.axis_index(ROW) * n_col + lax.axis_index(COL)) * slim
    row_ids = lax.broadcasted_iota(jnp.int32, (slim, regions), 0)
    col_ids = lax.broadcasted_iota(jnp.int32, (slim, regions), 1)
    diagonal = jnp.where(col_ids == row_ids + first_row, prior_precision[0][:, None], 0.0)
    h0 = product(0, 0) + p10.astype(jnp.float32) + diagonal
    h2 = product(0, 2)
    bands = jnp.stack([h0, h1, h2])

    panel = contract_last(
        coupling, lax.all_gather(pivot_solve, (ROW, COL), axis=1, tiled=True)
    ).astype(jnp.bfloat16)
    gram = contract_last(panel, gather(panel[None], 1, False, 1)[0])
    term = jnp.where(week == 1, h0, 0.0) - gram
    schur = lax.psum_scatter(
        term.astype(jnp.bfloat16), "week", scatter_dimension=1, tiled=True
    ).astype(jnp.float32)
    return (bands[None], panel, schur)


def solution(mesh):
    placed = (
        P("week", None, None, (ROW, COL)),
        P("week", None),
        P("week", None),
        P("week", (ROW, COL)),
        P("week", (ROW, COL)),
    )
    return jax.shard_map(
        body,
        mesh=mesh,
        in_specs=placed,
        out_specs=(
            P("week", None, (ROW, COL), None),
            P((ROW, COL), "week"),
            P((ROW, COL), "week"),
        ),
        check_vma=False,
    )
```

time: 968 us -> 669 us (0.69)
  waiting for transfers between devices: 818 us -> 298 us
  Pallas kernels: 0 us -> 236 us
  other arithmetic: 56.3 us -> 32.7 us
    all_gather x3 -> x1, waiting for transfers between devices: 637 us -> 0.01 us  [body(): lax.all_gather(pivot_solve, (ROW, COL), axis=1, tiled=True)]
    pallas_call x0 -> x2, Pallas kernels: none -> 236 us  [gather(): pl.pallas_call(functools.partial(gather_kernel, n_row, n_col, axis, by_we...]
    ppermute x2 -> x5, waiting for transfers between devices: 1.42 us -> 212 us  [send(): return lax.ppermute(block.astype(jnp.bfloat16), 'week', moves)]
    psum x1 -> x0, waiting for transfers between devices: 136 us -> none  [spread(): return lax.psum(jnp.where(mine, shard, jnp.zeros_like(shard)), axis)]
    reduce_scatter x1, waiting for transfers between devices: 42.7 us -> 85.4 us  [body(): lax.psum_scatter(term.astype(jnp.bfloat16), 'week', scatter_dimension=1,...]
    scatter-add x3 -> x0, other arithmetic: 29.3 us -> none  [the longest x1 14.8 us: body(): bands = partial_blocks[0:lags].at[:lags - 1].add(carried[0])]
    convert_element_type x0 -> x2, other arithmetic: none -> 18.1 us  [the longest x1 9.32 us: body(): term.astype(jnp.bfloat16)]
    another operation x2 -> x0, other arithmetic: 17.7 us -> none  [products(): return jnp.stack(result)]
  transfers between devices with their start and end apart: 7 -> 7, of which waited for: 6 -> 2; matrix products, arithmetic and copies ran while one was open for 10% -> 15% of each run, Pallas kernels for 0% -> 35%
where the time goes in v1:
time: 669 us; the launch traced here: 668 us
  waiting for transfers between devices  298 us (45%)
  Pallas kernels  236 us (35%)
  matrix products  76.9 us (11%)
  other arithmetic  32.7 us (5%)
  between operations  14.2 us (2%)
  starting transfers between devices  10.7 us (2%)
    pallas_call x2, Pallas kernels, gather(): pl.pallas_call(functools.partial(gather_kernel, n_row, n_col, axis, by_we...  236 us
    ppermute x5, waiting for transfers between devices, send(): return lax.ppermute(block.astype(jnp.bfloat16), 'week', moves)  212 us
    reduce_scatter x1, waiting for transfers between devices, body(): lax.psum_scatter(term.astype(jnp.bfloat16), 'week', scatter_dimension=1,...  85.4 us
    dot_general x6, matrix products, contract_first(): lax.dot_general(left, right, (((0,), (0,)), ((), ())), preferred_element_...  59.4 us
    dot_general x2, matrix products, contract_last(): lax.dot_general(left, right, (((1,), (1,)), ((), ())), preferred_element_...  17.4 us
  transfers between devices with their start and end apart: 7, of which 2 were waited for; matrix products, arithmetic and copies ran while one was open for 15% of the time, Pallas kernels for 35%

profile of v1, /device:TPU:0, one launch (start us, length us, event | category | flops | bytes accessed | tf_op | source)
XLA Modules:
  0.0 668.5 jit_solution(52259019683033601)
XLA Ops:
  7.2 0.0 all-gather.2.cloned.1.call-start
  7.2 0.7 all-gather.2.cloned.1.call-update
  7.9 0.0 reduce-scatter.2.cloned.1.call-start
  8.0 165.8 %shard_map.76 = bf16[3,1024,4096]{2,1,0:T(8,128)(2,1)} custom-call(bf16[3,1024,512]{2,1,0:T(8,128)(2,1)} %bitcast.64), custom_call_target="tpu_custom_call" | custom-call | bytes 176160768 | tf_op jit(solution)/shard_map/pallas_call | solution.py:153
  173.9 9.7 %select_convert_fusion.1 = bf16[512,4096]{1,0:T(8,128)(2,1)} fusion(bf16[3,1024,4096]{2,1,0:T(8,128)(2,1)} %shard_map.76, pred[]{:T(512)S(6)} %ge.53, f32[1024]{0:T(1024)S(1)} %bitcast.67, bf16[1,3,1024,512]{3,2,1,0:T(8,128)(2,1)S(1)} %copy-done.1), kind=kOutput, calls=%fused_computation.19 | convolution fusion | flops 4300734464 | bytes 13635585 | tf_op jit(solution)/shard_map/dot_general | solution.py:173
  183.6 2.6 collective-permute-start.2
  186.2 11.1 %select_convert_fusion.3 = (bf16[512,4096]{1,0:T(8,128)(2,1)}, f32[512,4096]{1,0:T(8,128)}) fusion(pred[]{:T(512)S(6)} %ge.51, bf16[3,1024,4096]{2,1,0:T(8,128)(2,1)} %shard_map.76, f32[1024]{0:T(1024)S(1)} %bitcast.70, bf16[1,3,1024,512]{3,2,1,0:T(8,128)(2,1)S(1)} %copy-done.1), kind=kOutput, calls=%fused_computation.25 | convolution fusion | flops 4298637312 | bytes 22024192 | tf_op jit(solution)/shard_map/dot_general | solution.py:173
  197.3 2.6 collective-permute-start.3
  199.9 9.8 %select_convert_fusion.2 = bf16[512,4096]{1,0:T(8,128)(2,1)} fusion(bf16[3,1024,4096]{2,1,0:T(8,128)(2,1)} %shard_map.76, pred[]{:T(512)S(6)} %ge.53, bf16[1,3,1024,512]{3,2,1,0:T(8,128)(2,1)S(1)} %copy-done.1, f32[1024]{0:T(1024)S(1)} %bitcast.68), kind=kOutput, calls=%fused_computation.23 | convolution fusion | flops 4300734464 | bytes 13635585 | tf_op jit(solution)/shard_map/dot_general | solution.py:173
  209.7 2.6 collective-permute-start
  212.3 8.8 %select_convert_fusion = (bf16[512,4096]{1,0:T(8,128)(2,1)}, f32[1,512,4096]{2,1,0:T(8,128)}) fusion(bf16[512,4096]{1,0:T(8,128)(2,1)} %select_convert_fusion.1, bf16[512,4096]{1,0:T(8,128)(2,1)} %collective-permute-done.3, bf16[512,4096]{1,0:T(8,128)(2,1)} %collective-permute-done.2, f32[512,4096]{1,0:T(8,128)} %get-tuple-element.11, pred[]{:T(512)S(6)} %eq.12, ...), kind=kLoop, calls=%fused_computation.16 | loop fusion | flops 16777216 | bytes 33554432 | tf_op jit(solution)/shard_map/convert_element_type | solution.py:206
  221.1 1.5 collective-permute-start.4
  222.6 10.8 %add_convert_fusion = bf16[512,4096]{1,0:T(8,128)(2,1)} fusion(bf16[512,4096]{1,0:T(8,128)(2,1)} %collective-permute-done, bf16[3,1024,4096]{2,1,0:T(8,128)(2,1)} %shard_map.76, pred[]{:T(512)S(6)} %ge.51, f32[1024]{0:T(1024)S(1)} %bitcast.71, bf16[1,3,1024,512]{3,2,1,0:T(8,128)(2,1)S(1)} %copy-done.1), kind=kOutput, calls=%fused_computation.22 | convolution fusion | flops 4304928768 | bytes 17829888 | tf_op jit(solution)/shard_map/dot_general | solution.py:173
  233.4 1.3 collective-permute-start.1
  234.7 10.4 %fusion.12 = f32[512,4096]{1,0:T(8,128)} fusion(bf16[3,1024,4096]{2,1,0:T(8,128)(2,1)} %shard_map.76, f32[1024]{0:T(1024)S(1)} %bitcast.66, bf16[1,3,1024,512]{3,2,1,0:T(8,128)(2,1)S(1)} %copy-done.1), kind=kOutput, calls=%fused_computation.13 | convolution fusion | flops 4296540160 | bytes 17829888 | tf_op jit(solution)/shard_map/dot_general | solution.py:173
  245.0 212.1 %collective-permute-done.4 = bf16[512,4096]{1,0:T(8,128)(2,1)} collective-permute-done((bf16[512,4096]{1,0:T(8,128)(2,1)}, bf16[512,4096]{1,0:T(8,128)(2,1)}, u32[]{:S(2)}, u32[]{:S(2)}) %collective-permute-start.4) | collective-permute-done | bytes 4194336 | tf_op jit(solution)/shard_map/ppermute | solution.py:169
  457.2 10.2 %fusion.39 = bf16[512,1024]{1,0:T(8,128)(2,1)} fusion(bf16[1024,4096]{1,0:T(8,128)(2,1)} %all-gather.2.cloned.1.call-done, bf16[512,4096]{1,0:T(8,128)(2,1)} %collective-permute-done.4, bf16[512,4096]{1,0:T(8,128)(2,1)} %get-tuple-element.5, pred[]{:T(512)S(6)} %or.3), kind=kOutput, calls=%fused_computation.48 | convolution fusion | flops 4299685888 | bytes 17825792 | tf_op jit(solution)/shard_map/dot_general | solution.py:179
  467.4 69.9 %shard_map.77 = bf16[1,4096,1024]{2,1,0:T(8,128)(2,1)} custom-call(bf16[1,512,1024]{2,1,0:T(8,128)(2,1)} %bitcast.65), custom_call_target="tpu_custom_call" | custom-call | bytes 58720256 | tf_op jit(solution)/shard_map/pallas_call | solution.py:153
  537.3 7.3 %fusion = f32[512,4096]{1,0:T(8,128)S(1)} fusion(bf16[512,1024]{1,0:T(8,128)(2,1)} %fusion.39, bf16[1,4096,1024]{2,1,0:T(8,128)(2,1)} %shard_map.77), kind=kOutput, calls=%fused_computation.1 | convolution fusion | flops 4294967296 | bytes 17825792 | tf_op jit(solution)/shard_map/dot_general | solution.py:179
  544.6 9.3 %subtract_convert_fusion = (bf16[512,4096]{1,0:T(8,128)(2,1)}, f32[1,512,4096]{2,1,0:T(8,128)}) fusion(f32[512,4096]{1,0:T(8,128)S(1)} %fusion, pred[]{:T(512)S(6)} %eq.12, f32[512]{0:T(512)S(1)} %bitcast.72, s32[512]{0:T(512)S(1)} %iota_add_fusion, bf16[512,4096]{1,0:T(8,128)(2,1)} %collective-permute-done.1, f32[512,4096]{1,0:T(8,128)} %fusion.12, pred[]{:T(512)S(6)} %ge.48), kind=kLoop, calls=%fused_computation.15 | loop fusion | flops 18874368 | bytes 33558528 | tf_op jit(solution)/shard_map/convert_element_type | solution.py:229
  553.9 7.7 %select_bitcast_fusion = f32[1,512,4096]{2,1,0:T(8,128)S(1)} fusion(bf16[3,1024,4096]{2,1,0:T(8,128)(2,1)} %shard_map.76, pred[]{:T(512)S(6)} %ge.53, f32[1024]{0:T(1024)S(1)} %bitcast.69, bf16[1,3,1024,512]{3,2,1,0:T(8,128)(2,1)S(1)} %copy-done.1), kind=kOutput, calls=%fused_computation.17 | convolution fusion | flops 4298637312 | bytes 17829888 | tf_op jit(solution)/shard_map/dot_general | solution.py:173
  561.7 11.8 %maximum_bitcast_fusion = f32[1,3,512,4096]{3,2,1,0:T(8,128)} fusion(f32[1,512,4096]{2,1,0:T(8,128)S(1)} %select_bitcast_fusion, f32[1,512,4096]{2,1,0:T(8,128)} %get-tuple-element.6, f32[1,512,4096]{2,1,0:T(8,128)S(1)} %copy-done), kind=kLoop, calls=%fused_computation | loop fusion | flops 12582912 | bytes 50331648 | tf_op jit(solution)/shard_map/broadcast_in_dim | solution.py:231
  573.4 85.4 %reduce-scatter.2.cloned.1.call-done = bf16[512,1024]{1,0:T(8,128)(2,1)} async-done(((bf16[512,4096]{1,0:T(8,128)(2,1)}), bf16[512,1024]{1,0:T(8,128)(2,1)}) %reduce-scatter.2.cloned.1.call-update) | async-done | bytes 1048592 | tf_op jit(solution)/shard_map/reduce_scatter | solution.py:228
  658.8 2.8 convert_element_type.122
  (18 shorter events, 0.1 us)
Async XLA Ops:
  7.2 450.0 %all-gather.2.cloned.1.call-start = ((), (), s32[]{:S(2)}) async-start(), calls=%async_computation.1 | async-start | bytes 9437184 | tf_op jit(solution)/shard_map/all_gather | solution.py:224
  7.9 650.9 %reduce-scatter.2.cloned.1.call-start = ((), (), s32[]{:S(2)}) async-start(), calls=%async_computation.2 | async-start | bytes 5242880 | tf_op jit(solution)/shard_map/reduce_scatter | solution.py:228
  8.0 165.9 %copy-start.2 = (f32[1,1024]{1,0:T(1,128)S(1)}, f32[1,1024]{1,0:T(1,128)}, u32[]{:S(2)}) copy-start(f32[1,1024]{1,0:T(1,128)} %param.7) | copy-start | bytes 12292
  8.0 165.9 %copy-start.3 = (s32[1,1024]{1,0:T(1,128)S(1)}, s32[1,1024]{1,0:T(1,128)}, u32[]{:S(2)}) copy-start(s32[1,1024]{1,0:T(1,128)} %param.6) | copy-start | bytes 12292
  8.0 165.9 %copy-start.1 = (bf16[1,3,1024,512]{3,2,1,0:T(8,128)(2,1)S(1)}, bf16[1,3,1024,512]{3,2,1,0:T(8,128)(2,1)}, u32[]{:S(2)}) copy-start(bf16[1,3,1024,512]{3,2,1,0:T(8,128)(2,1)} %param.5) | copy-start | bytes 9437188
  183.6 28.7 %collective-permute-start.2 = (bf16[512,4096]{1,0:T(8,128)(2,1)}, bf16[512,4096]{1,0:T(8,128)(2,1)}, u32[]{:S(2)}, u32[]{:S(2)}) collective-permute-start(bf16[512,4096]{1,0:T(8,128)(2,1)} %select_convert_fusion.1), channel_id=1, source_target_pairs={{16,8},{24,16},{17,9},{25,17},{18,10},{26,18},{19,11},{27,19},{20,... | collective-permute-start | bytes 12582920 | tf_op jit(solution)/shard_map/ppermute | solution.py:169
  197.3 15.0 %collective-permute-start.3 = (bf16[512,4096]{1,0:T(8,128)(2,1)}, bf16[512,4096]{1,0:T(8,128)(2,1)}, u32[]{:S(2)}, u32[]{:S(2)}) collective-permute-start(bf16[512,4096]{1,0:T(8,128)(2,1)} %get-tuple-element.10), channel_id=1, source_target_pairs={{8,16},{9,17},{10,18},{11,19},{12,20},{13,21},{14,22},{15,23}} | collective-permute-start | bytes 12582920 | tf_op jit(solution)/shard_map/ppermute | solution.py:169
  209.7 12.9 %collective-permute-start = (bf16[512,4096]{1,0:T(8,128)(2,1)}, bf16[512,4096]{1,0:T(8,128)(2,1)}, u32[]{:S(2)}, u32[]{:S(2)}) collective-permute-start(bf16[512,4096]{1,0:T(8,128)(2,1)} %select_convert_fusion.2), channel_id=1, source_target_pairs={{16,8},{24,16},{17,9},{25,17},{18,10},{26,18},{19,11},{27,19},{20,... | collective-permute-start | bytes 12582920 | tf_op jit(solution)/shard_map/ppermute | solution.py:169
  221.1 236.1 %collective-permute-start.4 = (bf16[512,4096]{1,0:T(8,128)(2,1)}, bf16[512,4096]{1,0:T(8,128)(2,1)}, u32[]{:S(2)}, u32[]{:S(2)}) collective-permute-start(bf16[512,4096]{1,0:T(8,128)(2,1)} %get-tuple-element.5), channel_id=1, source_target_pairs={{16,24},{8,0},{17,25},{9,1},{18,26},{10,2},{19,27},{11,3},{20,28},... | collective-permute-start | bytes 12582920 | tf_op jit(solution)/shard_map/ppermute | solution.py:169
  233.4 311.2 %collective-permute-start.1 = (bf16[512,4096]{1,0:T(8,128)(2,1)}, bf16[512,4096]{1,0:T(8,128)(2,1)}, u32[]{:S(2)}, u32[]{:S(2)}) collective-permute-start(bf16[512,4096]{1,0:T(8,128)(2,1)} %add_convert_fusion), channel_id=1, source_target_pairs={{8,0},{16,8},{24,16},{9,1},{17,9},{25,17},{10,2},{18,10},{26,18},{... | collective-permute-start | bytes 12582920 | tf_op jit(solution)/shard_map/ppermute | solution.py:169
  537.3 7.3 %copy-start.4 = (f32[1,512]{1,0:T(1,128)S(1)}, f32[1,512]{1,0:T(1,128)}, u32[]{:S(2)}) copy-start(f32[1,512]{1,0:T(1,128)} %param.8) | copy-start | bytes 6148
  553.9 7.7 %copy-start = (f32[1,512,4096]{2,1,0:T(8,128)S(1)}, f32[1,512,4096]{2,1,0:T(8,128)}, u32[]{:S(2)}) copy-start(f32[1,512,4096]{2,1,0:T(8,128)} %get-tuple-element.4) | copy-start | bytes 25165828
Sparse Core Ops, SparseCore 0:
  10.0 214.7 all-gather.1
  554.1 104.7 reduce-scatter.1
